TPU v7x, 32 devices: a whole 2x2x4 slice. The times are simulated.
32 devices in a mesh: tm: 4 (over y, core), dom: 8 (over z, x).
Axes of the slice: x: 2, y: 2, z: 4, core: 2. Of those that a mesh axis runs over, the one named last changes fastest.
Arguments:
- particles: float32 [4, 64, 4096], P('tm', None, 'dom'), may hold values from -12 to 12, as said below
- noise: float32 [4, 64, 4096], P('tm', None, 'dom'), may hold values from -6 to 6
Outputs:
- advanced: float32 [4, 64, 4096], P('tm', None, 'dom')
Inputs may be any that keep to these rules, and one draw needn't show every extreme that they name: `particles`: positions of cells in principal components, each time point about a shifted centre.
All inputs are finite; a program needn't handle non-finite values.
Results may differ from a plain program's by a relative error of at most 0.012.
The roundings to bfloat16 on the way count: a program that leaves them out, or rounds other values in their place, can miss the bound.
Values may be sent and summed in bfloat16 or wider, within the bound.
A program may use at most 64 MiB of HBM per device.

v0:
```python
import functools
import math

import jax
import jax.numpy as jnp
from jax import lax
from jax.experimental import pallas as pl
from jax.experimental.pallas import tpu as pltpu
from jax.sharding import PartitionSpec as P

SWEEPS = 2
EPS = 4.0
STEP = 0.5
TEMP = 0.05
MESH = pl.DeviceIdType.MESH
EXTRA = 16
PIECE = 64
CHUNK = 512
LAG = 4


def crossed(me, i, n):
    total = 0
    bit = 1
    while bit < n:
        mine, its = (me // bit) % 2, (i // bit) % 2
        total = total + bit * (mine + its - 2 * mine * its)
        bit *= 2
    return total


def kernel(
    times, n, points_ref, noise_ref, out_ref,
    own, nxt, prv, npot, ppot, spot, tpot, xa, ya, yb, sa, sb, pw, m_ref, l_ref, acc,
    own_s, own_r, nxt_s, nxt_r, prv_s, prv_r, npot_s, npot_r, ppot_s, ppot_r,
):
    t = lax.axis_index("tm")
    me = lax.axis_index("dom")
    dim, width = points_ref.shape
    has_next = t < times - 1
    has_prev = t > 0
    low = 2 if n > 1 else 1
    log_count = EPS * math.log(n * width)

    points = points_ref[...]
    rounded = points.astype(jnp.bfloat16)
    own[me] = rounded
    xa[pl.ds(0, dim), :] = (rounded.astype(jnp.float32) * (1.0 / EPS)).astype(jnp.bfloat16)
    rows = lax.broadcasted_iota(jnp.int32, (EXTRA, width), 0)
    xa[pl.ds(dim, EXTRA), :] = jnp.where(rows < 3, 1.0 / EPS, 0.0).astype(jnp.bfloat16)

    barrier = pltpu.get_barrier_semaphore()
    same = [i for i in range(1, n) if i % low == 0 or i == 1]
    for i in same:
        pl.semaphore_signal(barrier, inc=1, device_id=(t, crossed(me, i, n)), device_id_type=MESH)

    @pl.when(has_next)
    def _():
        pl.semaphore_signal(barrier, inc=1, device_id=(t + 1, me), device_id_type=MESH)

    @pl.when(has_prev)
    def _():
        pl.semaphore_signal(barrier, inc=1, device_id=(t - 1, me), device_id_type=MESH)

    sides = has_next.astype(jnp.int32) + has_prev.astype(jnp.int32)
    pl.semaphore_wait(barrier, len(same) + sides)

    def own_copy(i, block, slot):
        return pltpu.make_async_remote_copy(
            src_ref=own.at[block], dst_ref=own.at[block], send_sem=own_s.at[slot], recv_sem=own_r.at[block],
            device_id=(t, crossed(me, i, n)), device_id_type=MESH)

    def to_prev(block):
        return pltpu.make_async_remote_copy(
            src_ref=own.at[block], dst_ref=nxt.at[block], send_sem=nxt_s.at[block], recv_sem=nxt_r.at[block],
            device_id=(t - 1, me), device_id_type=MESH)

    def to_next(block):
        return pltpu.make_async_remote_copy(
            src_ref=own.at[block], dst_ref=prv.at[block], send_sem=prv_s.at[block], recv_sem=prv_r.at[block],
            device_id=(t + 1, me), device_id_type=MESH)

    for i in range(low, n, low):
        own_copy(i, me, i).start()

    def pass_on(i):
        block = crossed(me, i, n)
        if i > 0:
            own_copy(i if i % low == 0 else 1, block, 0).wait_recv()
        if i % low == 0 and low > 1:
            own_copy(1, block, i + 1).start()

        @pl.when(has_prev)
        def _():
            to_prev(block).start()

        @pl.when(has_next)
        def _():
            to_next(block).start()

    order = [0]
    for i in range(low, n, low):
        order += [i, i - low + 1] if low > 1 else [i]
    if low > 1:
        order.append(n - 1)
    def extend(y_ref, block_ref, pot):
        y_ref[pl.ds(0, dim), :] = block_ref[...]
        high = pot.astype(jnp.bfloat16).astype(jnp.float32)
        rest = pot - high
        middle = rest.astype(jnp.bfloat16).astype(jnp.float32)
        least = rest - middle
        pieces = jnp.where(rows == 0, high, jnp.where(rows == 1, middle, jnp.where(rows == 2, least, 0.0)))
        y_ref[pl.ds(dim, EXTRA), :] = pieces.astype(jnp.bfloat16)

    def folded(values, join):
        parts = [values[r:r + 8] for r in range(0, values.shape[0], 8)]
        while len(parts) > 1:
            parts = [join(parts[k], parts[k + 1]) for k in range(0, len(parts) - 1, 2)] + (
                [parts[-1]] if len(parts) % 2 else [])
        return parts[0]

    def reset():
        m_ref[...] = jnp.full_like(m_ref, -jnp.inf)
        l_ref[...] = jnp.zeros_like(l_ref)

    def step(y_ref, new_scores, old_scores, old_block, mean):
        m_old = m_ref[...]
        highest, total = None, None
        if old_scores is not None:
            for start in range(0, width, PIECE):
                here = pl.ds(start, PIECE)
                weights = jnp.exp(old_scores[here, :] - m_old)
                part = folded(weights, jnp.add)
                total = part if total is None else total + part
                if mean:
                    pw[here, :] = weights.astype(jnp.bfloat16)
        if new_scores is not None:
            for start in range(0, width, CHUNK):
                here = pl.ds(start, CHUNK)
                scores = lax.dot_general(
                    y_ref[:, here], xa[...], (((0,), (0,)), ((), ())), preferred_element_type=jnp.float32)
                new_scores[here, :] = scores
                top = folded(scores, jnp.maximum)
                highest = top if highest is None else jnp.maximum(highest, top)
        if old_scores is not None:
            sums = l_ref[...] + jnp.sum(total, axis=0, keepdims=True)
            if mean:
                for start in range(0, width, CHUNK):
                    here = pl.ds(start, CHUNK)
                    acc[...] += lax.dot_general(
                        old_block[:, here], pw[here, :], (((1,), (0,)), ((), ())),
                        preferred_element_type=jnp.float32)
        else:
            sums = l_ref[...]
        if new_scores is not None:
            m_new = jnp.maximum(m_old, jnp.max(highest, axis=0, keepdims=True))
            scale = jnp.exp(m_old - m_new)
            m_ref[...] = m_new
            sums = sums * scale
            if mean and old_scores is not None:
                acc[...] = acc[...] * scale
        l_ref[...] = sums

    def sweep_over(prepare, slots, mean):
        def do(i, y_ref, new, old):
            prepare(y_ref, i)
            step(y_ref, new, old, slots.at[crossed(me, i - 1, n)], mean)

        prepare(ya, 0)
        step(ya, sa, None, None, mean)
        if n > 2:
            @pl.loop(0, n // 2 - 1)
            def _(h):
                do(2 * h + 1, yb, sb, sa)
                do(2 * h + 2, ya, sa, sb)
        do(n - 1, yb, sb, sa)
        step(None, None, sb, slots.at[crossed(me, n - 1, n)], mean)

    def result():
        return -EPS * (m_ref[...] + jnp.log(l_ref[...])) + log_count

    def spot_copy(sweep, i):
        return pltpu.make_async_remote_copy(
            src_ref=spot.at[sweep], dst_ref=ppot.at[sweep, me], send_sem=ppot_s.at[sweep, i],
            recv_sem=ppot_r.at[sweep, me], device_id=(t + 1, crossed(me, i, n)), device_id_type=MESH)

    def tpot_copy(sweep, i):
        return pltpu.make_async_remote_copy(
            src_ref=tpot.at[sweep], dst_ref=npot.at[sweep, me], send_sem=npot_s.at[sweep, i],
            recv_sem=npot_r.at[sweep, me], device_id=(t - 1, crossed(me, i, n)), device_id_type=MESH)

    def await_ppot(sweep, block):
        pltpu.make_async_remote_copy(
            src_ref=spot.at[sweep], dst_ref=ppot.at[sweep, block], send_sem=ppot_s.at[sweep, 0],
            recv_sem=ppot_r.at[sweep, block], device_id=(t - 1, block), device_id_type=MESH).wait_recv()

    def await_npot(sweep, block):
        pltpu.make_async_remote_copy(
            src_ref=tpot.at[sweep], dst_ref=npot.at[sweep, block], send_sem=npot_s.at[sweep, 0],
            recv_sem=npot_r.at[sweep, block], device_id=(t + 1, block), device_id_type=MESH).wait_recv()

    def landed(block, slots, sends, recvs):
        pltpu.make_async_remote_copy(
            src_ref=own.at[block], dst_ref=slots.at[block], send_sem=sends.at[block], recv_sem=recvs.at[block],
            device_id=(t, me), device_id_type=MESH).wait_recv()

    def send_source(sweep):
        spot[sweep] = result()
        for i in reversed(range(n)):
            spot_copy(sweep, i).start()

    def first_prepare(y_ref, i):
        block = crossed(me, i, n)
        landed(block, nxt, nxt_s, nxt_r)
        extend(y_ref, nxt.at[block], -0.5 * jnp.sum(
            jnp.square(nxt[block].astype(jnp.float32)), axis=0, keepdims=True))

    @pl.when(has_next)
    def _():
        reset()

    def first_step(k):
        @pl.when(has_next)
        def _():
            y_ref, new, old = (ya, sa, sb) if k % 2 == 0 else (yb, sb, sa)
            first_prepare(y_ref, order[k])
            step(y_ref, new, old if k > 0 else None, None, False)

    for k in range(n):
        pass_on(order[k])
        if k >= LAG:
            first_step(k - LAG)
    for k in range(max(0, n - LAG), n):
        first_step(k)

    @pl.when(has_next)
    def _():
        step(None, None, sb if n % 2 == 0 else sa, None, False)
        send_source(0)

    def source_pass(sweep):
        def prepare(y_ref, i):
            block = crossed(me, i, n)
            await_npot(sweep - 1, block)
            extend(y_ref, nxt.at[block], npot[sweep - 1, block])

        @pl.when(has_next)
        def _():
            reset()
            sweep_over(prepare, nxt, False)
            send_source(sweep)

    def target_pass(sweep):
        def prepare(y_ref, i):
            block = crossed(me, i, n)
            if sweep == 0:
                landed(block, prv, prv_s, prv_r)
            await_ppot(sweep, block)
            extend(y_ref, prv.at[block], ppot[sweep, block])

        @pl.when(has_prev)
        def _():
            reset()
            mean = sweep == SWEEPS - 1
            if mean:
                acc[...] = jnp.zeros_like(acc)
            sweep_over(prepare, prv, mean)
            tpot[sweep] = result()
            for i in reversed(range(n)):
                tpot_copy(sweep, i).start()

    for sweep in range(SWEEPS):
        if sweep > 0:
            source_pass(sweep)
        target_pass(sweep)

    @pl.when(has_prev)
    def _():
        out_ref[...] = points_ref[...] - STEP * (points_ref[...] - acc[...] / l_ref[...]) + (
            math.sqrt(2.0 * STEP * TEMP) * noise_ref[...])

    @pl.when(jnp.logical_not(has_prev))
    def _():
        out_ref[...] = points_ref[...] + math.sqrt(2.0 * STEP * TEMP) * noise_ref[...]

    @pl.when(has_next)
    def _():
        reset()
        acc[...] = jnp.zeros_like(acc)

        def prepare(y_ref, i):
            block = crossed(me, i, n)
            await_npot(SWEEPS - 1, block)
            extend(y_ref, nxt.at[block], npot[SWEEPS - 1, block])

        sweep_over(prepare, nxt, True)
        out_ref[...] = out_ref[...] - STEP * (points_ref[...] - acc[...] / l_ref[...])

    for i in range(low, n, low):
        own_copy(i, me, i).wait_send()
    if low > 1:
        for i in range(0, n, low):
            own_copy(1, crossed(me, i, n), i + 1).wait_send()

    @pl.when(has_prev)
    def _():
        for i in range(n):
            to_prev(i).wait_send()
            for sweep in range(SWEEPS):
                tpot_copy(sweep, i).wait_send()

    @pl.when(has_next)
    def _():
        for i in range(n):
            to_next(i).wait_send()
            for sweep in range(SWEEPS):
                spot_copy(sweep, i).wait_send()


def per_device(times, n, particles, noise):
    points = particles[0]
    dim, width = points.shape
    dma = pltpu.SemaphoreType.DMA
    row = (1, width)
    advanced = pl.pallas_call(
        functools.partial(kernel, times, n),
        out_shape=jax.ShapeDtypeStruct((dim, width), jnp.float32),
        in_specs=[pl.BlockSpec(memory_space=pltpu.VMEM)] * 2,
        out_specs=pl.BlockSpec(memory_space=pltpu.VMEM),
        scratch_shapes=[
            pltpu.VMEM((n, dim, width), jnp.bfloat16),
            pltpu.VMEM((n, dim, width), jnp.bfloat16),
            pltpu.VMEM((n, dim, width), jnp.bfloat16),
            pltpu.VMEM((SWEEPS, n) + row, jnp.float32),
            pltpu.VMEM((SWEEPS, n) + row, jnp.float32),
            pltpu.VMEM((SWEEPS,) + row, jnp.float32),
            pltpu.VMEM((SWEEPS,) + row, jnp.float32),
            pltpu.VMEM((dim + EXTRA, width), jnp.bfloat16),
            pltpu.VMEM((dim + EXTRA, width), jnp.bfloat16),
            pltpu.VMEM((dim + EXTRA, width), jnp.bfloat16),
            pltpu.VMEM((width, width), jnp.float32),
            pltpu.VMEM((width, width), jnp.float32),
            pltpu.VMEM((width, width), jnp.bfloat16),
            pltpu.VMEM(row, jnp.float32),
            pltpu.VMEM(row, jnp.float32),
            pltpu.VMEM((dim, width), jnp.float32),
            dma((n,)), dma((n,)), dma((n,)), dma((n,)), dma((n,)), dma((n,)),
            dma((SWEEPS, n)), dma((SWEEPS, n)), dma((SWEEPS, n)), dma((SWEEPS, n)),
        ],
        compiler_params=pltpu.CompilerParams(collective_id=0, has_side_effects=True),
    )(points, noise[0])
    return advanced[None]


def solution(mesh):
    times, n = mesh.shape["tm"], mesh.shape["dom"]
    assert n & (n - 1) == 0
    spec = P("tm", None, "dom")
    return jax.shard_map(
        functools.partial(per_device, times, n), mesh=mesh, in_specs=(spec, spec), out_specs=spec, check_vma=False)
```

profile of v0, /device:TPU:1, one launch (start us, length us, event | category | flops | bytes accessed | tf_op | source)
XLA Modules:
  0.0 48.0 jit_solution(5901135697203723570)
XLA Ops:
  0.0 46.4 %shard_map.28 = f32[64,512]{1,0:T(8,128)} custom-call(f32[64,512]{1,0:T(8,128)} %bitcast.4, f32[64,512]{1,0:T(8,128)} %bitcast.5), custom_call_target="tpu_custom_call" | custom-call | tf_op jit(solution)/shard_map/pallas_call | solution.py:325
  46.5 1.6 %copy.4 = f32[1,64,512]{2,1,0:T(8,128)} copy(f32[1,64,512]{2,1,0:T(8,128)} %bitcast.3) | data formatting | bytes 262144
where the time goes:
time: 48.2 us; the launch traced here: 48 us
  Pallas kernels  46.4 us (96%)
  local copies, waits for them, and re-layouts  1.57 us (3%)
    pallas_call x1, Pallas kernels, per_device(): pl.pallas_call(functools.partial(kernel, times, n), out_shape=jax.ShapeDt...  46.4 us
    unnamed x1, local copies, waits for them, and re-layouts  1.57 us

commit v1 on v0

--- a/solution.py
+++ b/solution.py
@@ -17,6 +17,8 @@
 PIECE = 64
 CHUNK = 512
 LAG = 4
+TILE = 128
+LANES = 128
 
 
 def crossed(me, i, n):
@@ -29,10 +31,21 @@
     return total
 
 
+def split3(value):
+    high = value.astype(jnp.bfloat16).astype(jnp.float32)
+    rest = value - high
+    middle = rest.astype(jnp.bfloat16).astype(jnp.float32)
+    return high, middle, rest - middle
+
+
+def dot(a, b, dims):
+    return lax.dot_general(a, b, (dims, ((), ())), preferred_element_type=jnp.float32)
+
+
 def kernel(
     times, n, points_ref, noise_ref, out_ref,
-    own, nxt, prv, npot, ppot, spot, tpot, xa, ya, yb, sa, sb, pw, m_ref, l_ref, acc,
-    own_s, own_r, nxt_s, nxt_r, prv_s, prv_r, npot_s, npot_r, ppot_s, ppot_r,
+    own, nxt, prv, lall, lown, ppot, spot, xa, xt, ya, yb, yx, y2, kept, gam, csum, pair, sa, sb, pw, m_ref, l_ref, acc, wide,
+    own_s, own_r, nxt_s, nxt_r, prv_s, prv_r, lall_s, lall_r, ppot_s, ppot_r,
 ):
     t = lax.axis_index("tm")
     me = lax.axis_index("dom")
@@ -40,7 +53,7 @@
     has_next = t < times - 1
     has_prev = t > 0
     low = 2 if n > 1 else 1
-    log_count = EPS * math.log(n * width)
+    half = max(n // 2, 1)
 
     points = points_ref[...]
     rounded = points.astype(jnp.bfloat16)
@@ -103,13 +116,11 @@
         order += [i, i - low + 1] if low > 1 else [i]
     if low > 1:
         order.append(n - 1)
-    def extend(y_ref, block_ref, pot):
+    def extend(y_ref, block_ref, pot, ones):
         y_ref[pl.ds(0, dim), :] = block_ref[...]
-        high = pot.astype(jnp.bfloat16).astype(jnp.float32)
-        rest = pot - high
-        middle = rest.astype(jnp.bfloat16).astype(jnp.float32)
-        least = rest - middle
-        pieces = jnp.where(rows == 0, high, jnp.where(rows == 1, middle, jnp.where(rows == 2, least, 0.0)))
+        high, middle, least = split3(pot)
+        tail = jnp.where((rows >= 3) & (rows < 6), ones, 0.0)
+        pieces = jnp.where(rows == 0, high, jnp.where(rows == 1, middle, jnp.where(rows == 2, least, tail)))
         y_ref[pl.ds(dim, EXTRA), :] = pieces.astype(jnp.bfloat16)
 
     def folded(values, join):
@@ -176,44 +187,51 @@
         do(n - 1, yb, sb, sa)
         step(None, None, sb, slots.at[crossed(me, n - 1, n)], mean)
 
-    def result():
-        return -EPS * (m_ref[...] + jnp.log(l_ref[...])) + log_count
-
-    def spot_copy(sweep, i):
+    def spot_copy(i):
         return pltpu.make_async_remote_copy(
-            src_ref=spot.at[sweep], dst_ref=ppot.at[sweep, me], send_sem=ppot_s.at[sweep, i],
-            recv_sem=ppot_r.at[sweep, me], device_id=(t + 1, crossed(me, i, n)), device_id_type=MESH)
-
-    def tpot_copy(sweep, i):
+            src_ref=spot, dst_ref=ppot.at[me], send_sem=ppot_s.at[i],
+            recv_sem=ppot_r.at[me], device_id=(t + 1, crossed(me, i, n)), device_id_type=MESH)
+
+    def await_ppot(block):
+        pltpu.make_async_remote_copy(
+            src_ref=spot, dst_ref=ppot.at[block], send_sem=ppot_s.at[0],
+            recv_sem=ppot_r.at[block], device_id=(t - 1, block), device_id_type=MESH).wait_recv()
+
+    def sum_copy(sweep, part, i, block):
+        some = pl.ds(part * half, half)
         return pltpu.make_async_remote_copy(
-            src_ref=tpot.at[sweep], dst_ref=npot.at[sweep, me], send_sem=npot_s.at[sweep, i],
-            recv_sem=npot_r.at[sweep, me], device_id=(t - 1, crossed(me, i, n)), device_id_type=MESH)
-
-    def await_ppot(sweep, block):
-        pltpu.make_async_remote_copy(
-            src_ref=spot.at[sweep], dst_ref=ppot.at[sweep, block], send_sem=ppot_s.at[sweep, 0],
-            recv_sem=ppot_r.at[sweep, block], device_id=(t - 1, block), device_id_type=MESH).wait_recv()
-
-    def await_npot(sweep, block):
-        pltpu.make_async_remote_copy(
-            src_ref=tpot.at[sweep], dst_ref=npot.at[sweep, block], send_sem=npot_s.at[sweep, 0],
-            recv_sem=npot_r.at[sweep, block], device_id=(t + 1, block), device_id_type=MESH).wait_recv()
+            src_ref=lown.at[sweep, some], dst_ref=lall.at[sweep, block, some], send_sem=lall_s.at[sweep, part, i],
+            recv_sem=lall_r.at[sweep, part, block], device_id=(t, crossed(me, i, n)), device_id_type=MESH)
+
+    def send_sums(sweep, part):
+        some = pl.ds(part * half, half)
+        lown[sweep, some] = gam[some] + jnp.log(csum[some])
+        for i in reversed(range(1, n)):
+            sum_copy(sweep, part, i, me).start()
+
+    def factors(sweep):
+        for i in range(1, n):
+            for part in range(n // half):
+                sum_copy(sweep, part, 0, crossed(me, i, n)).wait_recv()
+        lall[sweep, me] = lown[sweep]
+        top = lall[sweep, 0]
+        for k in range(1, n):
+            top = jnp.maximum(top, lall[sweep, k])
+        total = jnp.exp(lall[sweep, 0] - top)
+        for k in range(1, n):
+            total = total + jnp.exp(lall[sweep, k] - top)
+        return jnp.exp(gam[...] - (top + jnp.log(total)))
 
     def landed(block, slots, sends, recvs):
         pltpu.make_async_remote_copy(
             src_ref=own.at[block], dst_ref=slots.at[block], send_sem=sends.at[block], recv_sem=recvs.at[block],
             device_id=(t, me), device_id_type=MESH).wait_recv()
 
-    def send_source(sweep):
-        spot[sweep] = result()
-        for i in reversed(range(n)):
-            spot_copy(sweep, i).start()
-
     def first_prepare(y_ref, i):
         block = crossed(me, i, n)
         landed(block, nxt, nxt_s, nxt_r)
         extend(y_ref, nxt.at[block], -0.5 * jnp.sum(
-            jnp.square(nxt[block].astype(jnp.float32)), axis=0, keepdims=True))
+            jnp.square(nxt[block].astype(jnp.float32)), axis=0, keepdims=True), 1.0)
 
     @pl.when(has_next)
     def _():
@@ -222,7 +240,8 @@
     def first_step(k):
         @pl.when(has_next)
         def _():
-            y_ref, new, old = (ya, sa, sb) if k % 2 == 0 else (yb, sb, sa)
+            new, old = (sa, sb) if k % 2 == 0 else (sb, sa)
+            y_ref = yx.at[crossed(me, order[k], n)]
             first_prepare(y_ref, order[k])
             step(y_ref, new, old if k > 0 else None, None, False)
 
@@ -236,46 +255,70 @@
     @pl.when(has_next)
     def _():
         step(None, None, sb if n % 2 == 0 else sa, None, False)
-        send_source(0)
-
-    def source_pass(sweep):
+        shift = -(m_ref[...] + jnp.log(l_ref[...]))
+        m_ref[...] = shift
+        high, middle, least = split3(shift)
+        xa[pl.ds(dim, EXTRA), :] = jnp.where(rows < 3, 1.0 / EPS, jnp.where(rows == 3, high, jnp.where(
+            rows == 4, middle, jnp.where(rows == 5, least, 0.0)))).astype(jnp.bfloat16)
+        xt[...] = xa[...].astype(jnp.float32).T.astype(jnp.bfloat16)
+
+        for b in range(n):
+            new = sa if b % 2 == 0 else sb
+            cols = pl.ds(b * width, width)
+            top = None
+            for start in range(0, width, TILE):
+                here = pl.ds(start, TILE)
+                scores = dot(xt[here, :], yx[b], ((1,), (0,)))
+                new[here, :] = scores
+                part = folded(scores, jnp.maximum)
+                top = part if top is None else jnp.maximum(top, part)
+            top = jnp.max(top, axis=0, keepdims=True)
+            total = None
+            for start in range(0, width, TILE):
+                here = pl.ds(start, TILE)
+                weights = jnp.exp(new[here, :] - top)
+                kept[here, cols] = weights.astype(jnp.bfloat16)
+                part = folded(weights, jnp.add)
+                total = part if total is None else total + part
+            gam[pl.ds(b, 1), :] = top
+            csum[pl.ds(b, 1), :] = jnp.sum(total, axis=0, keepdims=True)
+            if (b + 1) % half == 0:
+                send_sums(0, b // half)
+
+        scale = factors(0)
+        high = scale.astype(jnp.bfloat16)
+        pair[pl.ds(0, n), :] = high.astype(jnp.float32)
+        pair[pl.ds(n, n), :] = scale - high.astype(jnp.float32)
+        both = pair[...].astype(jnp.bfloat16)
+        row = lax.broadcasted_iota(jnp.int32, (2 * n, width), 0)
+        total = jnp.zeros((2 * n, width), jnp.float32)
+        for b in range(n):
+            part = dot(both, kept[:, pl.ds(b * width, width)], ((1,), (1,)))
+            total = total + jnp.where((row == b) | (row == n + b), part, 0.0)
+        total = jnp.sum(total, axis=0, keepdims=True)
+        spot[...] = EPS * (m_ref[...] - jnp.log(total))
+        for i in reversed(range(n)):
+            spot_copy(i).start()
+        ratio = 1.0 / total
+        high = ratio.astype(jnp.bfloat16).astype(jnp.float32)
+        both = jnp.where(rows == 0, high, jnp.where(rows == 1, ratio - high, 0.0)).astype(jnp.bfloat16)
+        for b in range(n):
+            part = dot(both, kept[:, pl.ds(b * width, width)], ((1,), (0,)))
+            csum[pl.ds(b, 1), :] = jnp.sum(part, axis=0, keepdims=True)
+            if (b + 1) % half == 0:
+                send_sums(1, b // half)
+
+    @pl.when(has_prev)
+    def _():
         def prepare(y_ref, i):
             block = crossed(me, i, n)
-            await_npot(sweep - 1, block)
-            extend(y_ref, nxt.at[block], npot[sweep - 1, block])
-
-        @pl.when(has_next)
-        def _():
-            reset()
-            sweep_over(prepare, nxt, False)
-            send_source(sweep)
-
-    def target_pass(sweep):
-        def prepare(y_ref, i):
-            block = crossed(me, i, n)
-            if sweep == 0:
-                landed(block, prv, prv_s, prv_r)
-            await_ppot(sweep, block)
-            extend(y_ref, prv.at[block], ppot[sweep, block])
-
-        @pl.when(has_prev)
-        def _():
-            reset()
-            mean = sweep == SWEEPS - 1
-            if mean:
-                acc[...] = jnp.zeros_like(acc)
-            sweep_over(prepare, prv, mean)
-            tpot[sweep] = result()
-            for i in reversed(range(n)):
-                tpot_copy(sweep, i).start()
-
-    for sweep in range(SWEEPS):
-        if sweep > 0:
-            source_pass(sweep)
-        target_pass(sweep)
-
-    @pl.when(has_prev)
-    def _():
+            landed(block, prv, prv_s, prv_r)
+            await_ppot(block)
+            extend(y_ref, prv.at[block], ppot[block], 0.0)
+
+        reset()
+        acc[...] = jnp.zeros_like(acc)
+        sweep_over(prepare, prv, True)
         out_ref[...] = points_ref[...] - STEP * (points_ref[...] - acc[...] / l_ref[...]) + (
             math.sqrt(2.0 * STEP * TEMP) * noise_ref[...])
 
@@ -285,16 +328,19 @@
 
     @pl.when(has_next)
     def _():
-        reset()
-        acc[...] = jnp.zeros_like(acc)
-
-        def prepare(y_ref, i):
-            block = crossed(me, i, n)
-            await_npot(SWEEPS - 1, block)
-            extend(y_ref, nxt.at[block], npot[SWEEPS - 1, block])
-
-        sweep_over(prepare, nxt, True)
-        out_ref[...] = out_ref[...] - STEP * (points_ref[...] - acc[...] / l_ref[...])
+        gam[...] = factors(1)
+        side = dim + EXTRA
+        lane = wide.shape[1] // 2
+        y2[...] = jnp.zeros_like(y2)
+        for b in range(n):
+            scaled = yx[b].astype(jnp.float32) * gam[pl.ds(b, 1), :]
+            high = scaled.astype(jnp.bfloat16)
+            y2[b % 2, pl.ds(0, side), :] = high
+            y2[b % 2, pl.ds(lane, side), :] = (scaled - high.astype(jnp.float32)).astype(jnp.bfloat16)
+            part = dot(kept[:, pl.ds(b * width, width)], y2[b % 2], ((1,), (1,)))
+            wide[...] = part if b == 0 else wide[...] + part
+        mean = (wide[:, pl.ds(0, lane)] + wide[:, pl.ds(lane, lane)]).T
+        out_ref[...] = out_ref[...] - STEP * (points_ref[...] - mean[:dim] / mean[dim + 3:dim + 4])
 
     for i in range(low, n, low):
         own_copy(i, me, i).wait_send()
@@ -306,15 +352,16 @@
     def _():
         for i in range(n):
             to_prev(i).wait_send()
-            for sweep in range(SWEEPS):
-                tpot_copy(sweep, i).wait_send()
 
     @pl.when(has_next)
     def _():
         for i in range(n):
             to_next(i).wait_send()
-            for sweep in range(SWEEPS):
-                spot_copy(sweep, i).wait_send()
+            spot_copy(i).wait_send()
+        for sweep in range(SWEEPS):
+            for part in range(n // half):
+                for i in range(1, n):
+                    sum_copy(sweep, part, i, me).wait_send()
 
 
 def per_device(times, n, particles, noise):
@@ -322,6 +369,8 @@
     dim, width = points.shape
     dma = pltpu.SemaphoreType.DMA
     row = (1, width)
+    tall = dim + EXTRA
+    lanes = -(-tall // LANES) * LANES
     advanced = pl.pallas_call(
         functools.partial(kernel, times, n),
         out_shape=jax.ShapeDtypeStruct((dim, width), jnp.float32),
@@ -331,21 +380,29 @@
             pltpu.VMEM((n, dim, width), jnp.bfloat16),
             pltpu.VMEM((n, dim, width), jnp.bfloat16),
             pltpu.VMEM((n, dim, width), jnp.bfloat16),
-            pltpu.VMEM((SWEEPS, n) + row, jnp.float32),
-            pltpu.VMEM((SWEEPS, n) + row, jnp.float32),
-            pltpu.VMEM((SWEEPS,) + row, jnp.float32),
-            pltpu.VMEM((SWEEPS,) + row, jnp.float32),
-            pltpu.VMEM((dim + EXTRA, width), jnp.bfloat16),
-            pltpu.VMEM((dim + EXTRA, width), jnp.bfloat16),
-            pltpu.VMEM((dim + EXTRA, width), jnp.bfloat16),
+            pltpu.VMEM((SWEEPS, n, n, width), jnp.float32),
+            pltpu.VMEM((SWEEPS, n, width), jnp.float32),
+            pltpu.VMEM((n,) + row, jnp.float32),
+            pltpu.VMEM(row, jnp.float32),
+            pltpu.VMEM((tall, width), jnp.bfloat16),
+            pltpu.VMEM((width, tall), jnp.bfloat16),
+            pltpu.VMEM((tall, width), jnp.bfloat16),
+            pltpu.VMEM((tall, width), jnp.bfloat16),
+            pltpu.VMEM((n, tall, width), jnp.bfloat16),
+            pltpu.VMEM((2, 2 * lanes, width), jnp.bfloat16),
+            pltpu.VMEM((width, n * width), jnp.bfloat16),
+            pltpu.VMEM((n, width), jnp.float32),
+            pltpu.VMEM((n, width), jnp.float32),
+            pltpu.VMEM((2 * n, width), jnp.float32),
             pltpu.VMEM((width, width), jnp.float32),
             pltpu.VMEM((width, width), jnp.float32),
             pltpu.VMEM((width, width), jnp.bfloat16),
             pltpu.VMEM(row, jnp.float32),
             pltpu.VMEM(row, jnp.float32),
             pltpu.VMEM((dim, width), jnp.float32),
+            pltpu.VMEM((width, 2 * lanes), jnp.float32),
             dma((n,)), dma((n,)), dma((n,)), dma((n,)), dma((n,)), dma((n,)),
-            dma((SWEEPS, n)), dma((SWEEPS, n)), dma((SWEEPS, n)), dma((SWEEPS, n)),
+            dma((SWEEPS, 2, n)), dma((SWEEPS, 2, n)), dma((n,)), dma((n,)),
         ],
         compiler_params=pltpu.CompilerParams(collective_id=0, has_side_effects=True),
     )(points, noise[0])

time: 48.2 us -> 39 us (0.81)
  the two profiles are of different devices: /device:TPU:1 before, /device:TPU:0 now
where the time goes in v1:
time: 39 us; the launch traced here: 38.9 us
  Pallas kernels  37.3 us (96%)
  local copies, waits for them, and re-layouts  1.57 us (4%)
    pallas_call x1, Pallas kernels, per_device(): pl.pallas_call(functools.partial(kernel, times, n), out_shape=jax.ShapeDt...  37.3 us
    unnamed x1, local copies, waits for them, and re-layouts  1.57 us

profile of v1, /device:TPU:0, one launch (start us, length us, event | category | flops | bytes accessed | tf_op | source)
XLA Modules:
  0.0 38.9 jit_solution(14286514093312027426)
XLA Ops:
  0.0 37.3 %shard_map.28 = f32[64,512]{1,0:T(8,128)} custom-call(f32[64,512]{1,0:T(8,128)} %bitcast.4, f32[64,512]{1,0:T(8,128)} %bitcast.5), custom_call_target="tpu_custom_call" | custom-call | tf_op jit(solution)/shard_map/pallas_call | solution.py:374
  37.3 1.6 %copy.4 = f32[1,64,512]{2,1,0:T(8,128)} copy(f32[1,64,512]{2,1,0:T(8,128)} %bitcast.3) | data formatting | bytes 262144

commit v2 on v1

--- a/solution.py
+++ b/solution.py
@@ -16,7 +16,7 @@
 EXTRA = 16
 PIECE = 64
 CHUNK = 512
-LAG = 4
+LAG = 1
 TILE = 128
 LANES = 128
 
@@ -44,78 +44,95 @@
 
 def kernel(
     times, n, points_ref, noise_ref, out_ref,
-    own, nxt, prv, lall, lown, ppot, spot, xa, xt, ya, yb, yx, y2, kept, gam, csum, pair, sa, sb, pw, m_ref, l_ref, acc, wide,
-    own_s, own_r, nxt_s, nxt_r, prv_s, prv_r, lall_s, lall_r, ppot_s, ppot_r,
+    points, noise, own, nxt, prv, lall, lown, ppot, spot, xa, xt, ya, yb, yx, y2, kept, gam, csum, pair, sa, sb, pw,
+    m_ref, l_ref, acc, wide, load, nxt_s, nxt_r, prv_s, prv_r, row_s, side_s, near_s, lall_s, lall_r, ppot_s, ppot_r,
 ):
     t = lax.axis_index("tm")
     me = lax.axis_index("dom")
-    dim, width = points_ref.shape
+    dim, width = points.shape
     has_next = t < times - 1
     has_prev = t > 0
     low = 2 if n > 1 else 1
     half = max(n // 2, 1)
 
-    points = points_ref[...]
-    rounded = points.astype(jnp.bfloat16)
-    own[me] = rounded
+    loads = [pltpu.make_async_copy(points_ref, points, load.at[0]), pltpu.make_async_copy(noise_ref, noise, load.at[1])]
+    for copy in loads:
+        copy.start()
+    row_ids = range(0, n, low)
+    barrier = pltpu.get_barrier_semaphore()
+
+    def greet(*device):
+        pl.semaphore_signal(barrier, inc=1, device_id=device, device_id_type=MESH)
+
+    if low > 1:
+        greet(t, crossed(me, 1, n))
+
+    @pl.when(has_next)
+    def _():
+        for i in row_ids:
+            greet(t + 1, crossed(me, i, n))
+
+    @pl.when(t >= 2)
+    def _():
+        greet(t - 2, me)
+
+    @pl.when(t == 1)
+    def _():
+        for i in row_ids:
+            greet(0, crossed(me, i, n))
+
+    loads[0].wait()
+    rounded = points[...].astype(jnp.bfloat16)
+    own[...] = rounded
     xa[pl.ds(0, dim), :] = (rounded.astype(jnp.float32) * (1.0 / EPS)).astype(jnp.bfloat16)
     rows = lax.broadcasted_iota(jnp.int32, (EXTRA, width), 0)
     xa[pl.ds(dim, EXTRA), :] = jnp.where(rows < 3, 1.0 / EPS, 0.0).astype(jnp.bfloat16)
 
-    barrier = pltpu.get_barrier_semaphore()
-    same = [i for i in range(1, n) if i % low == 0 or i == 1]
-    for i in same:
-        pl.semaphore_signal(barrier, inc=1, device_id=(t, crossed(me, i, n)), device_id_type=MESH)
-
-    @pl.when(has_next)
-    def _():
-        pl.semaphore_signal(barrier, inc=1, device_id=(t + 1, me), device_id_type=MESH)
+    pl.semaphore_wait(barrier, low - 1 + len(row_ids) + (t < times - 2).astype(jnp.int32))
+
+    def to_row(slots, sends, recvs, i, step):
+        return pltpu.make_async_remote_copy(
+            src_ref=own, dst_ref=slots.at[me], send_sem=sends.at[i], recv_sem=recvs.at[me],
+            device_id=(t + step, crossed(me, i, n)), device_id_type=MESH)
+
+    def to_side(slots, sends, recvs, block):
+        return pltpu.make_async_remote_copy(
+            src_ref=slots.at[block], dst_ref=slots.at[block], send_sem=sends.at[block], recv_sem=recvs.at[block],
+            device_id=(t, crossed(me, 1, n)), device_id_type=MESH)
+
+    def to_after(block):
+        return pltpu.make_async_remote_copy(
+            src_ref=nxt.at[block], dst_ref=prv.at[block], send_sem=prv_s.at[block], recv_sem=prv_r.at[block],
+            device_id=(t + 2, me), device_id_type=MESH)
+
+    row_order = [0] + list(reversed(row_ids[1:]))
+    order = row_order + [i + 1 for i in row_order if low > 1]
 
     @pl.when(has_prev)
     def _():
-        pl.semaphore_signal(barrier, inc=1, device_id=(t - 1, me), device_id_type=MESH)
-
-    sides = has_next.astype(jnp.int32) + has_prev.astype(jnp.int32)
-    pl.semaphore_wait(barrier, len(same) + sides)
-
-    def own_copy(i, block, slot):
-        return pltpu.make_async_remote_copy(
-            src_ref=own.at[block], dst_ref=own.at[block], send_sem=own_s.at[slot], recv_sem=own_r.at[block],
-            device_id=(t, crossed(me, i, n)), device_id_type=MESH)
-
-    def to_prev(block):
-        return pltpu.make_async_remote_copy(
-            src_ref=own.at[block], dst_ref=nxt.at[block], send_sem=nxt_s.at[block], recv_sem=nxt_r.at[block],
-            device_id=(t - 1, me), device_id_type=MESH)
-
-    def to_next(block):
-        return pltpu.make_async_remote_copy(
-            src_ref=own.at[block], dst_ref=prv.at[block], send_sem=prv_s.at[block], recv_sem=prv_r.at[block],
-            device_id=(t + 1, me), device_id_type=MESH)
-
-    for i in range(low, n, low):
-        own_copy(i, me, i).start()
-
-    def pass_on(i):
+        for i in row_order:
+            to_row(nxt, nxt_s, nxt_r, i, -1).start()
+
+    def pass_on(k):
+        i = order[k]
         block = crossed(me, i, n)
-        if i > 0:
-            own_copy(i if i % low == 0 else 1, block, 0).wait_recv()
-        if i % low == 0 and low > 1:
-            own_copy(1, block, i + 1).start()
-
-        @pl.when(has_prev)
-        def _():
-            to_prev(block).start()
 
         @pl.when(has_next)
         def _():
-            to_next(block).start()
-
-    order = [0]
-    for i in range(low, n, low):
-        order += [i, i - low + 1] if low > 1 else [i]
-    if low > 1:
-        order.append(n - 1)
+            landed(block, nxt, nxt_s, nxt_r)
+            if i % low == 0 and low > 1:
+                to_side(nxt, side_s, nxt_r, block).start()
+
+        @pl.when(t < times - 2)
+        def _():
+            to_after(block).start()
+
+        if k == len(row_order) - 1:
+            @pl.when(t == 0)
+            def _():
+                for i in row_order:
+                    to_row(prv, row_s, prv_r, i, 1).start()
+
     def extend(y_ref, block_ref, pot, ones):
         y_ref[pl.ds(0, dim), :] = block_ref[...]
         high, middle, least = split3(pot)
@@ -224,12 +241,11 @@
 
     def landed(block, slots, sends, recvs):
         pltpu.make_async_remote_copy(
-            src_ref=own.at[block], dst_ref=slots.at[block], send_sem=sends.at[block], recv_sem=recvs.at[block],
+            src_ref=slots.at[block], dst_ref=slots.at[block], send_sem=sends.at[block], recv_sem=recvs.at[block],
             device_id=(t, me), device_id_type=MESH).wait_recv()
 
     def first_prepare(y_ref, i):
         block = crossed(me, i, n)
-        landed(block, nxt, nxt_s, nxt_r)
         extend(y_ref, nxt.at[block], -0.5 * jnp.sum(
             jnp.square(nxt[block].astype(jnp.float32)), axis=0, keepdims=True), 1.0)
 
@@ -246,7 +262,7 @@
             step(y_ref, new, old if k > 0 else None, None, False)
 
     for k in range(n):
-        pass_on(order[k])
+        pass_on(k)
         if k >= LAG:
             first_step(k - LAG)
     for k in range(max(0, n - LAG), n):
@@ -285,6 +301,14 @@
             if (b + 1) % half == 0:
                 send_sums(0, b // half)
 
+        if low > 1:
+            @pl.when(t == 1)
+            def _():
+                for i in row_order:
+                    block = crossed(me, i, n)
+                    landed(block, prv, prv_s, prv_r)
+                    to_side(prv, near_s, prv_r, block).start()
+
         scale = factors(0)
         high = scale.astype(jnp.bfloat16)
         pair[pl.ds(0, n), :] = high.astype(jnp.float32)
@@ -308,23 +332,29 @@
             if (b + 1) % half == 0:
                 send_sums(1, b // half)
 
+    loads[1].wait()
+
     @pl.when(has_prev)
     def _():
         def prepare(y_ref, i):
             block = crossed(me, i, n)
-            landed(block, prv, prv_s, prv_r)
             await_ppot(block)
             extend(y_ref, prv.at[block], ppot[block], 0.0)
+
+        for i in order:
+            @pl.when(jnp.logical_or(t > 1, i % low == 1 or low == 1))
+            def _():
+                landed(crossed(me, i, n), prv, prv_s, prv_r)
 
         reset()
         acc[...] = jnp.zeros_like(acc)
         sweep_over(prepare, prv, True)
-        out_ref[...] = points_ref[...] - STEP * (points_ref[...] - acc[...] / l_ref[...]) + (
-            math.sqrt(2.0 * STEP * TEMP) * noise_ref[...])
+        out_ref[...] = points[...] - STEP * (points[...] - acc[...] / l_ref[...]) + (
+            math.sqrt(2.0 * STEP * TEMP) * noise[...])
 
     @pl.when(jnp.logical_not(has_prev))
     def _():
-        out_ref[...] = points_ref[...] + math.sqrt(2.0 * STEP * TEMP) * noise_ref[...]
+        out_ref[...] = points[...] + math.sqrt(2.0 * STEP * TEMP) * noise[...]
 
     @pl.when(has_next)
     def _():
@@ -340,23 +370,35 @@
             part = dot(kept[:, pl.ds(b * width, width)], y2[b % 2], ((1,), (1,)))
             wide[...] = part if b == 0 else wide[...] + part
         mean = (wide[:, pl.ds(0, lane)] + wide[:, pl.ds(lane, lane)]).T
-        out_ref[...] = out_ref[...] - STEP * (points_ref[...] - mean[:dim] / mean[dim + 3:dim + 4])
-
-    for i in range(low, n, low):
-        own_copy(i, me, i).wait_send()
+        out_ref[...] = out_ref[...] - STEP * (points[...] - mean[:dim] / mean[dim + 3:dim + 4])
+
+    @pl.when(has_prev)
+    def _():
+        for i in row_order:
+            to_row(nxt, nxt_s, nxt_r, i, -1).wait_send()
+
+    @pl.when(t == 0)
+    def _():
+        for i in row_order:
+            to_row(prv, row_s, prv_r, i, 1).wait_send()
+
+    @pl.when(t < times - 2)
+    def _():
+        for i in range(n):
+            to_after(i).wait_send()
+
     if low > 1:
-        for i in range(0, n, low):
-            own_copy(1, crossed(me, i, n), i + 1).wait_send()
-
-    @pl.when(has_prev)
-    def _():
+        @pl.when(t == 1)
+        def _():
+            for i in row_order:
+                to_side(prv, near_s, prv_r, crossed(me, i, n)).wait_send()
+
+    @pl.when(has_next)
+    def _():
+        if low > 1:
+            for i in row_order:
+                to_side(nxt, side_s, nxt_r, crossed(me, i, n)).wait_send()
         for i in range(n):
-            to_prev(i).wait_send()
-
-    @pl.when(has_next)
-    def _():
-        for i in range(n):
-            to_next(i).wait_send()
             spot_copy(i).wait_send()
         for sweep in range(SWEEPS):
             for part in range(n // half):
@@ -374,10 +416,12 @@
     advanced = pl.pallas_call(
         functools.partial(kernel, times, n),
         out_shape=jax.ShapeDtypeStruct((dim, width), jnp.float32),
-        in_specs=[pl.BlockSpec(memory_space=pltpu.VMEM)] * 2,
+        in_specs=[pl.BlockSpec(memory_space=pl.ANY)] * 2,
         out_specs=pl.BlockSpec(memory_space=pltpu.VMEM),
         scratch_shapes=[
-            pltpu.VMEM((n, dim, width), jnp.bfloat16),
+            pltpu.VMEM((dim, width), jnp.float32),
+            pltpu.VMEM((dim, width), jnp.float32),
+            pltpu.VMEM((dim, width), jnp.bfloat16),
             pltpu.VMEM((n, dim, width), jnp.bfloat16),
             pltpu.VMEM((n, dim, width), jnp.bfloat16),
             pltpu.VMEM((SWEEPS, n, n, width), jnp.float32),
@@ -401,7 +445,7 @@
             pltpu.VMEM(row, jnp.float32),
             pltpu.VMEM((dim, width), jnp.float32),
             pltpu.VMEM((width, 2 * lanes), jnp.float32),
-            dma((n,)), dma((n,)), dma((n,)), dma((n,)), dma((n,)), dma((n,)),
+            dma((2,)), dma((n,)), dma((n,)), dma((n,)), dma((n,)), dma((n,)), dma((n,)), dma((n,)),
             dma((SWEEPS, 2, n)), dma((SWEEPS, 2, n)), dma((n,)), dma((n,)),
         ],
         compiler_params=pltpu.CompilerParams(collective_id=0, has_side_effects=True),

time: 39 us -> 34.6 us (0.89)
  Pallas kernels: 37.3 us -> 32.9 us
    pallas_call x1, Pallas kernels: 37.3 us -> 32.9 us  [per_device(): pl.pallas_call(functools.partial(kernel, times, n), out_shape=jax.ShapeDt...]
where the time goes in v2:
time: 34.6 us; the launch traced here: 34.4 us
  Pallas kernels  32.9 us (95%)
  local copies, waits for them, and re-layouts  1.57 us (5%)
    pallas_call x1, Pallas kernels, per_device(): pl.pallas_call(functools.partial(kernel, times, n), out_shape=jax.ShapeDt...  32.9 us
    unnamed x1, local copies, waits for them, and re-layouts  1.57 us

profile of v2, /device:TPU:0, one launch (start us, length us, event | category | flops | bytes accessed | tf_op | source)
XLA Modules:
  0.0 34.4 jit_solution(8451133581207818826)
XLA Ops:
  0.0 32.9 %shard_map.28 = f32[64,512]{1,0:T(8,128)} custom-call(f32[64,512]{1,0:T(8,128)} %bitcast.4, f32[64,512]{1,0:T(8,128)} %bitcast.5), custom_call_target="tpu_custom_call" | custom-call | tf_op jit(solution)/shard_map/pallas_call | solution.py:416
  32.9 1.6 %copy.4 = f32[1,64,512]{2,1,0:T(8,128)} copy(f32[1,64,512]{2,1,0:T(8,128)} %bitcast.3) | data formatting | bytes 262144
